TPU v7x, 128 devices: a whole 4x4x4 slice. The times are simulated.
128 devices in a mesh: kv: 2 (over y_lo), ctx: 64 (over z, x, y_hi, core).
Axes of the slice: x: 4, y: 4 (y_hi: 2, y_lo: 2; y = y_hi * 2 + y_lo), z: 4, core: 2. Of those that a mesh axis runs over, the one named last changes fastest.
Arguments:
- residual: bfloat16 [64, 8192], P(None, 'ctx'), may hold values from -8 to 8
- queries: bfloat16 [64, 8192], P(None, 'kv'), may hold values from -16 to 16
- draft_token_keys: bfloat16 [64, 1024], P(None, 'kv'), may hold values from -32 to 32
- draft_token_values: bfloat16 [64, 1024], P(None, 'kv'), may hold values from -8 to 8
- cache_keys: bfloat16 [2, 32768, 1024], P(None, 'ctx', 'kv'), may hold values from -32 to 32
- cached_value_rows: bfloat16 [2, 32768, 1024], P(None, 'ctx', 'kv'), may hold values from -8 to 8
- tenant_ids: int32 [64], replicated, may hold values from 0 to 1, as said below
- tree_mask: int32 [64, 64], replicated, may hold values from 0 to 1, as said below
- cache_lengths: int32 [2], replicated, may hold values from 16385 to 32768
- out_weight: bfloat16 [8192, 8192], P('kv', 'ctx'), may hold values from -0.0625 to 0.0625
- out_signs: bfloat16 [2, 8192, 8192], P(None, 'kv', 'ctx'), may hold values from -1 to 1, as said below
- norm_gain: float32 [8192], P('ctx'), may hold values from 0.1 to 1.9
- gate_weight: bfloat16 [8192, 16384], P(None, ('kv', 'ctx')), may hold values from -0.0625 to 0.0625
- up_weight: bfloat16 [8192, 16384], P(None, ('kv', 'ctx')), may hold values from -0.0625 to 0.0625
- down_weight: bfloat16 [16384, 8192], P(('kv', 'ctx')), may hold values from -0.1875 to 0.1875
- gate_signs: bfloat16 [2, 8192, 16384], P(None, None, ('kv', 'ctx')), may hold values from -1 to 1, as said below
- up_signs: bfloat16 [2, 8192, 16384], P(None, None, ('kv', 'ctx')), may hold values from -1 to 1, as said below
- down_signs: bfloat16 [2, 16384, 8192], P(None, ('kv', 'ctx')), may hold values from -1 to 1, as said below
- delta_scale: float32 [2, 4], replicated, may hold values from 0.3 to 0.9
Outputs:
- mixed: bfloat16 [64, 8192], P(None, 'ctx')
Inputs may be any that keep to these rules, and one draw needn't show every extreme that they name: `tenant_ids`: exactly 32 tokens belong to each tenant. `tree_mask`: entry (i, j) is 1 exactly when token j is token i or an ancestor of token i in the draft tree of their common tenant; each tenant's 32 tokens form one tree. `out_signs`: every entry is 1 or -1. `gate_signs`: every entry is 1 or -1. `up_signs`: every entry is 1 or -1. `down_signs`: every entry is 1 or -1.
All inputs are finite; a program needn't handle non-finite values.
Results may differ from a plain program's by a relative error of at most 0.013.
Values may be sent and summed in bfloat16 or wider, within the bound.
A program may use at most 128 MiB of HBM per device.

v0:
```python
import jax
import jax.numpy as jnp
from jax import lax
from jax.sharding import PartitionSpec as P

D = 8192
QUERY_HEADS = 64
HEAD_SIZE = 128
FF = 16384
NEG = -1e30
EPS = 1e-05


def sent_together(arrays, axis, split_dim, concat_dim, along):
    columns = [a.reshape(*a.shape[:along], -1) for a in arrays]
    both = jnp.concatenate(columns, axis=along)
    filled, at, done = (
        lax.all_to_all(both, axis, split_axis=split_dim, concat_axis=concat_dim, tiled=True),
        0,
        [],
    )
    for a, column in zip(arrays, columns):
        share = filled[..., at : at + column.shape[along]]
        done.append(share.reshape(*share.shape[:along], *a.shape[along:]))
        at += column.shape[along]
    return tuple(done)


def sent_to_all(shard, axis):
    copies = jnp.broadcast_to(shard, (lax.axis_size(axis), *shard.shape))
    return lax.all_to_all(copies, axis, split_axis=0, concat_axis=0, tiled=True)


def laid_out(tiles, dim):
    tiles = jnp.moveaxis(tiles, 0, dim)
    shape = tiles.shape
    return tiles.reshape(*shape[:dim], shape[dim] * shape[dim + 1], *shape[dim + 2 :])


def collect(shard, axis, dim):
    tiles = sent_to_all(shard, axis)
    return laid_out(tiles, dim)


def of_everyone(shard, axis):
    return sent_to_all(shard, axis).astype(jnp.float32).sum(axis=0)


def of_everyone_2(shard, axis):
    everything = sent_to_all(shard, axis)
    return jnp.sum(everything, axis=0)


def cut_along(shard, dim, peers):
    before, after = (shard.shape[:dim], shard.shape[dim + 1 :])
    return jnp.moveaxis(shard.reshape(*before, peers, -1, *after), dim, 0)


def sum_at_owner(shard, axis, dim):
    tiles = cut_along(shard, dim, lax.axis_size(axis))
    arrived = lax.all_to_all(tiles, axis, split_axis=0, concat_axis=0, tiled=True)
    return arrived.sum(axis=0)


def combine(first, second):
    first_top, first_total, first_out = first
    second_top, second_total, second_out = second
    peak = jnp.maximum(first_top, second_top)
    first_scale = jnp.exp(first_top - peak)
    second_scale = jnp.exp(second_top - peak)
    total = first_total * first_scale + second_total * second_scale
    merged = first_out * first_scale[..., None] + second_out * second_scale[..., None]
    return (peak, total, merged)


def draft_rows(query_rows, group_rows, visible_rows, key_rows, value_rows, factor):
    groups = key_rows.shape[1]
    choose = (group_rows[:, None] == jnp.arange(groups, dtype=jnp.int32)[None, :]).astype(
        jnp.float32
    )
    every_group = (
        jnp.einsum("rd,kgd->rgk", query_rows, key_rows, preferred_element_type=jnp.float32) * factor
    )
    scores = jnp.einsum("rgk,rg->rk", every_group, choose, precision=lax.Precision.HIGHEST)
    masked = jnp.where(visible_rows, scores, NEG)
    peak = jnp.max(masked, axis=-1)
    weights = jnp.where(visible_rows, jnp.exp(masked - peak[:, None]), 0.0)
    total = jnp.sum(weights, axis=-1)
    every_value = jnp.einsum(
        "rk,kgd->rgd", weights.astype(jnp.bfloat16), value_rows, preferred_element_type=jnp.float32
    )
    result = jnp.einsum("rgd,rg->rd", every_value, choose, precision=lax.Precision.HIGHEST)
    return (peak, total, result)


def shards(
    residual,
    queries,
    draft_token_keys,
    draft_token_values,
    cache_keys,
    cached_value_rows,
    tenant_ids,
    tree_mask,
    cache_lengths,
    out_weight,
    out_signs,
    norm_gain,
    gate_weight,
    up_weight,
    down_weight,
    gate_signs,
    up_signs,
    down_signs,
    delta_scale,
):
    tenants = cache_keys.shape[0]
    tokens = tenant_ids.shape[0]
    draft = tokens // tenants
    heads_here = queries.shape[1] // HEAD_SIZE
    groups_here = draft_token_keys.shape[1] // HEAD_SIZE
    group_width = heads_here // groups_here
    ctx_rows = cache_keys.shape[1]
    factor = HEAD_SIZE ** (-0.5)
    sort_order = jnp.argsort(tenant_ids, stable=True)
    inverse = jnp.argsort(sort_order)
    sorted_queries = queries[sort_order]
    query_blocks = sorted_queries.reshape(tenants, draft, groups_here, group_width, HEAD_SIZE)
    draft_key_lines = draft_token_keys[sort_order].reshape(tokens, groups_here, HEAD_SIZE)
    draft_value_lines = draft_token_values[sort_order].reshape(tokens, groups_here, HEAD_SIZE)
    visible = tree_mask[sort_order][:, sort_order] > 0
    first_slot = lax.axis_index("ctx") * ctx_rows
    slot_ids = first_slot + jnp.arange(ctx_rows, dtype=jnp.int32)
    live = (slot_ids[None, :] < cache_lengths[:, None])[:, None, None, None, :]
    cache_key_blocks = cache_keys.reshape(tenants, ctx_rows, groups_here, HEAD_SIZE)
    cache_value_blocks = cached_value_rows.reshape(tenants, ctx_rows, groups_here, HEAD_SIZE)
    scores = (
        jnp.einsum(
            "tqgwd,tjgd->tqgwj", query_blocks, cache_key_blocks, preferred_element_type=jnp.float32
        )
        * factor
    )
    masked = jnp.where(live, scores, NEG)
    peak = jnp.max(masked, axis=-1)
    weights = jnp.where(live, jnp.exp(masked - peak[..., None]), 0.0)
    total = jnp.sum(weights, axis=-1)
    weighted = jnp.einsum(
        "tqgwj,tjgd->tqgwd",
        weights.astype(jnp.bfloat16),
        cache_value_blocks,
        preferred_element_type=jnp.float32,
    )
    part_top = peak.reshape(tokens, heads_here)
    part_total = total.reshape(tokens, heads_here)
    part_out = weighted.reshape(tokens, heads_here, HEAD_SIZE)
    n_ctx = lax.axis_size("ctx")
    all_rows = tokens * heads_here
    share = all_rows // n_ctx
    got_top, got_total, got_out = (
        lax.all_to_all(
            part_top.reshape(1, all_rows), "ctx", split_axis=1, concat_axis=0, tiled=True
        ),
        *sent_together(
            (part_total.reshape(1, all_rows), part_out.reshape(1, all_rows, HEAD_SIZE)),
            "ctx",
            1,
            0,
            2,
        ),
    )
    summit = jnp.max(got_top, axis=0)
    rescale = jnp.exp(got_top - summit)
    merged = (
        summit,
        jnp.sum(got_total * rescale, axis=0),
        jnp.sum(got_out * rescale[..., None], axis=0),
    )
    first_row = lax.axis_index("ctx") * share
    row_ids = first_row + jnp.arange(share, dtype=jnp.int32)
    token_rows = row_ids // heads_here
    group_rows = row_ids % heads_here // group_width
    query_rows = lax.dynamic_slice_in_dim(
        sorted_queries.reshape(all_rows, HEAD_SIZE), first_row, share, 0
    )
    own = draft_rows(
        query_rows, group_rows, visible[token_rows], draft_key_lines, draft_value_lines, factor
    )
    final_top, final_total, final_out = combine(merged, own)
    finished = (final_out / final_total[:, None]).astype(jnp.bfloat16)
    attention = collect(finished, "ctx", 0).reshape(tokens, heads_here * HEAD_SIZE)
    attention_split = attention.reshape(tenants, draft, -1)
    projected = jnp.dot(attention, out_weight, preferred_element_type=jnp.float32)
    out_delta = jnp.einsum(
        "tqh,thf->tqf", attention_split, out_signs, preferred_element_type=jnp.float32
    )
    projected = projected + (
        out_delta * (delta_scale[:, 0] * (QUERY_HEADS * HEAD_SIZE) ** (-0.5))[:, None, None]
    ).reshape(tokens, -1)
    summed_heads = of_everyone(projected.astype(jnp.bfloat16), "kv").astype(jnp.float32)
    hidden = residual[sort_order].astype(jnp.float32) + summed_heads
    squares = of_everyone_2(jnp.sum(hidden * hidden, axis=1), "ctx")
    normed = (hidden * lax.rsqrt(squares / D + EPS)[:, None] * norm_gain).astype(jnp.bfloat16)
    hidden_units = gate_weight.shape[1]
    piece = lax.all_gather(normed, "ctx", axis=1, tiled=True)
    size = piece.shape[1]
    split_piece = piece.reshape(tenants, draft, size)
    gate_base = jnp.dot(piece, gate_weight, preferred_element_type=jnp.float32)
    up_base = jnp.dot(piece, up_weight, preferred_element_type=jnp.float32)
    gate_delta = jnp.einsum(
        "tqf,tfh->tqh", split_piece, gate_signs, preferred_element_type=jnp.float32
    )
    up_delta = jnp.einsum("tqf,tfh->tqh", split_piece, up_signs, preferred_element_type=jnp.float32)
    gate = gate_base + (gate_delta * (delta_scale[:, 1] * D ** (-0.5))[:, None, None]).reshape(
        tokens, hidden_units
    )
    up_part = up_base + (up_delta * (delta_scale[:, 2] * D ** (-0.5))[:, None, None]).reshape(
        tokens, hidden_units
    )
    active = (jax.nn.silu(gate) * up_part).astype(jnp.bfloat16)
    active_split = active.reshape(tenants, draft, hidden_units)
    down_factor = delta_scale[:, 3] * FF ** (-0.5)
    features_here = residual.shape[1]
    base_part = lax.dot_general(
        down_weight, active, (((0,), (1,)), ((), ())), preferred_element_type=jnp.float32
    )
    delta_part = jnp.einsum(
        "thf,tqh->ftq", down_signs, active_split, preferred_element_type=jnp.float32
    )
    delta_part = delta_part * down_factor[None, :, None]
    lowered = sum_at_owner(
        base_part + delta_part.reshape(features_here * lax.axis_size("ctx"), tokens), "ctx", 0
    )
    lowered = of_everyone(lowered.astype(jnp.bfloat16), "kv").astype(jnp.float32)
    return (hidden + lowered.T).astype(jnp.bfloat16)[inverse]


def solution(mesh):
    return jax.shard_map(
        shards,
        mesh=mesh,
        in_specs=(
            P(None, "ctx"),
            P(None, "kv"),
            P(None, "kv"),
            P(None, "kv"),
            P(None, "ctx", "kv"),
            P(None, "ctx", "kv"),
            P(),
            P(),
            P(),
            P("kv", "ctx"),
            P(None, "kv", "ctx"),
            P("ctx"),
            P(None, ("kv", "ctx")),
            P(None, ("kv", "ctx")),
            P(("kv", "ctx"), None),
            P(None, None, ("kv", "ctx")),
            P(None, None, ("kv", "ctx")),
            P(None, ("kv", "ctx"), None),
            P(),
        ),
        out_specs=P(None, "ctx"),
        check_vma=False,
    )
```

profile of v0, /device:TPU:0, one launch (start us, length us, event | category | flops | bytes accessed | tf_op | source)
XLA Modules:
  0.0 268.2 jit_solution(5693490985125798498)
XLA Ops:
  6.5 2.8 %sort.34 = (s32[64]{0:T(128)}, s32[64]{0:T(128)S(1)}) sort(s32[64]{0:T(128)} %param.25, s32[64]{0:T(128)S(1)} %iota.25), dimensions={0}, to_apply=%region_0.0 | sort | flops 384 | bytes 1024 | tf_op jit(solution)/shard_map/jit(argsort)/sort | solution.py:125
  9.4 2.2 reshape.251
  11.6 0.9 gather_fusion.1
  12.6 4.0 %bitcast_reduce_fusion = (f32[2,32,4,8]{3,1,2,0:T(8,128)S(1)}, f32[2,4,32,8,512]{4,3,2,1,0:T(8,128)}) fusion(pred[2,512]{1,0:T(4,128)(4,1)S(1)} %broadcast_compare_fusion, bf16[2,512,4,128,1]{3,2,1,0,4:T(4,128)(2,1)} %bitcast.117, bf16[2,32,4,8,128]{4,3,2,1,0:T(8,128)(2,1)S(1)} %bitcast.119), kind=kOutput, calls=%fused_computation.12 | convolution fusion | flops 271579136 | bytes 5776384 | tf_op jit(solution)/shard_map/tqgwd,tjgd->tqgwj/dot_general | solution.py:138
  16.8 0.7 copy.96
  17.5 11.5 %all-to-all-start.1 = ((f32[1,64,32]{2,0,1:T(1,128)}), f32[1,64,32]{2,0,1:T(1,128)S(1)}, u32[]{:S(2)}, u32[]{:S(2)}) async-start(f32[1,64,32]{2,0,1:T(1,128)} %copy.96), calls=%async_computation.1 | async-start | bytes 65536 | tf_op jit(solution)/shard_map/all_to_all | solution.py:160
  29.0 1.0 reshape.254
  30.1 0.6 gather_fusion.2
  30.7 0.6 gather_fusion.3
  31.4 0.7 gather_fusion.5
  32.1 1.3 reshape.252
  33.5 3.5 %fusion.4 = f32[2,32,4,8]{3,1,2,0:T(8,128)S(1)} fusion(f32[2,4,32,8,512]{4,3,2,1,0:T(8,128)} %get-tuple-element.19, f32[2,32,4,8]{3,1,2,0:T(8,128)S(1)} %get-tuple-element.18, pred[2,512]{1,0:T(4,128)(4,1)S(1)} %broadcast_compare_fusion), kind=kLoop, calls=%fused_computation.17 | loop fusion | flops 5240832 | bytes 4211712 | tf_op jit(solution)/shard_map/reduce_sum | solution.py:146
  37.0 1.3 fusion.10
  38.3 0.1 copy.92
  38.5 1.3 reshape_reshape_reshape.8
  39.9 3.2 %pad_maximum_fusion = f32[1,2048,129]{2,1,0:T(8,128)} fusion(f32[1,2048,128]{2,1,0:T(8,128)S(1)} %bitcast.118, f32[1,2048,1]{2,1,0:T(8,128)} %reshape_reshape_reshape.8), kind=kLoop, calls=%fused_computation.19 | loop fusion | flops 264192 | bytes 2113536 | tf_op jit(solution)/shard_map/concatenate | solution.py:16
  43.1 0.8 fusion.13
  44.1 0.7 gather_fusion.6
  44.8 4.8 %copy.94 = f32[1,2048,129]{2,0,1:T(1,128)} copy(f32[1,2048,129]{2,1,0:T(8,128)} %pad_maximum_fusion) | data formatting | bytes 2113536 | tf_op jit(solution)/shard_map/concatenate | solution.py:16
  49.6 0.6 gather_fusion.4
  50.2 10.6 %all-to-all-start = ((f32[1,2048,129]{2,0,1:T(1,128)}), f32[1,2048,129]{2,0,1:T(1,128)}, u32[]{:S(2)}, u32[]{:S(2)}) async-start(f32[1,2048,129]{2,0,1:T(1,128)} %copy.94), calls=%async_computation | async-start | bytes 4194304 | tf_op jit(solution)/shard_map/all_to_all | solution.py:18
  60.9 0.3 fusion.31
  61.2 0.2 fusion.39
  61.4 0.2 fusion.24
  61.6 0.3 fusion.29
  62.1 28.9 %all-to-all-done = f32[1,2048,129]{2,0,1:T(1,128)} async-done(((f32[1,2048,129]{2,0,1:T(1,128)}), f32[1,2048,129]{2,0,1:T(1,128)}, u32[]{:S(2)}, u32[]{:S(2)}) %all-to-all-start) | async-done | bytes 1056800 | tf_op jit(solution)/shard_map/all_to_all | solution.py:18
  90.9 1.7 copy.118
  92.7 1.3 copy-done.4
  94.1 0.6 copy.103
  94.7 0.2 fusion.36
  95.0 2.2 fusion.17
  97.3 0.9 broadcast_in_dim.76
  98.2 5.5 %all-to-all-start.2 = ((bf16[64,32,128]{2,1,0:T(8,128)(2,1)}), bf16[64,32,128]{2,1,0:T(8,128)(2,1)S(1)}, u32[]{:S(2)}, u32[]{:S(2)}) async-start(bf16[64,32,128]{2,1,0:T(8,128)(2,1)} %broadcast_in_dim.76), calls=%async_computation.2 | async-start | bytes 1048576 | tf_op jit(solution)/shard_map/all_to_all | solution.py:31
  103.8 0.2 multiply_reduce_fusion.1
  104.0 13.7 %all-to-all-done.2 = bf16[64,32,128]{2,1,0:T(8,128)(2,1)S(1)} async-done(((bf16[64,32,128]{2,1,0:T(8,128)(2,1)}), bf16[64,32,128]{2,1,0:T(8,128)(2,1)S(1)}, u32[]{:S(2)}, u32[]{:S(2)}) %all-to-all-start.2) | async-done | bytes 524320 | tf_op jit(solution)/shard_map/all_to_all | solution.py:31
  117.7 0.2 reshape_reshape_reshape.7
  117.9 2.0 convolution_multiply_fusion.4
  120.0 1.6 fusion.16
  121.6 0.6 broadcast_in_dim.77
  122.2 3.3 %all-to-all-start.3 = ((bf16[2,64,128]{2,1,0:T(8,128)(2,1)}), bf16[2,64,128]{2,1,0:T(8,128)(2,1)S(1)}, u32[]{:S(2)}, u32[]{:S(2)}) async-start(bf16[2,64,128]{2,1,0:T(8,128)(2,1)} %broadcast_in_dim.77), calls=%async_computation.3 | async-start | bytes 65536 | tf_op jit(solution)/shard_map/all_to_all | solution.py:31
  125.5 0.6 gather_fusion
  126.1 3.2 %all-to-all-done.3 = bf16[2,64,128]{2,1,0:T(8,128)(2,1)S(1)} async-done(((bf16[2,64,128]{2,1,0:T(8,128)(2,1)}), bf16[2,64,128]{2,1,0:T(8,128)(2,1)S(1)}, u32[]{:S(2)}, u32[]{:S(2)}) %all-to-all-start.3) | async-done | bytes 32800 | tf_op jit(solution)/shard_map/all_to_all | solution.py:31
  129.5 13.8 %all_to_all.54 = f32[64,1,64]{2,1,0:T(1,128)S(1)} all-to-all(f32[64,1,64]{2,1,0:T(1,128)S(1)} %broadcast_in_dim.78), channel_id=1, replica_groups=mesh['kv'=2,'ctx'=64] {'ctx'}, dimensions={0} | all-to-all | bytes 32768 | tf_op jit(solution)/shard_map/all_to_all | solution.py:31
  143.4 0.7 multiply_convert_fusion
  144.1 57.7 %all-gather.2.cloned.1.call-done = bf16[64,8192]{1,0:T(8,128)(2,1)} async-done(((bf16[64,128]{1,0:T(8,128)(2,1)}), bf16[64,8192]{1,0:T(8,128)(2,1)}) %all-gather.2.cloned.1.call-update) | async-done | bytes 1048592 | tf_op jit(solution)/shard_map/all_gather | solution.py:204
  201.8 3.4 %convolution_multiply_fusion.2 = f32[2,32,128]{2,1,0:T(8,128)S(1)} fusion(bf16[2,32,8192]{2,1,0:T(8,128)(2,1)} %bitcast.109, bf16[2,8192,128]{2,1,0:T(8,128)(2,1)} %param.35, f32[2]{0:T(128)S(1)} %get-tuple-element.12), kind=kOutput, calls=%fused_computation.27 | convolution fusion | flops 134225920 | bytes 5275656 | tf_op jit(solution)/shard_map/tqf,tfh->tqh/dot_general | solution.py:212
  205.2 0.6 copy-done.5
  205.8 0.7 convolution_multiply_fusion.3
  206.6 0.3 copy-done.10
  206.9 0.5 convolution_add_fusion.1
  207.4 0.1 copy-done.11
  207.5 0.5 fusion.15
  208.0 1.0 copy-done.6
  209.0 0.7 convolution_multiply_fusion
  209.7 0.5 fusion.9
  210.2 1.6 copy.156
  211.8 8.6 %all-to-all-start.5 = ((f32[64,128,64]{1,2,0:T(8,128)}), f32[64,128,64]{1,2,0:T(8,128)}, u32[]{:S(2)}, u32[]{:S(2)}) async-start(f32[64,128,64]{1,2,0:T(8,128)} %bitcast.112), calls=%async_computation.5 | async-start | bytes 4194304 | tf_op jit(solution)/shard_map/all_to_all | solution.py:61
  220.4 2.0 sort.35
  222.4 28.1 %all-to-all-done.5 = f32[64,128,64]{1,2,0:T(8,128)} async-done(((f32[64,128,64]{1,2,0:T(8,128)}), f32[64,128,64]{1,2,0:T(8,128)}, u32[]{:S(2)}, u32[]{:S(2)}) %all-to-all-start.5) | async-done | bytes 2097184 | tf_op jit(solution)/shard_map/all_to_all | solution.py:61
  250.5 1.7 reduce_sum.88
  252.3 0.6 broadcast_in_dim.79
  252.9 3.3 %all-to-all-start.6 = ((bf16[2,128,64]{1,2,0:T(8,128)(2,1)}), bf16[2,128,64]{1,2,0:T(8,128)(2,1)S(1)}, u32[]{:S(2)}, u32[]{:S(2)}) async-start(bf16[2,128,64]{1,2,0:T(8,128)(2,1)} %broadcast_in_dim.79), calls=%async_computation.6 | async-start | bytes 65536 | tf_op jit(solution)/shard_map/all_to_all | solution.py:31
  256.2 3.9 %all-to-all-done.6 = bf16[2,128,64]{1,2,0:T(8,128)(2,1)S(1)} async-done(((bf16[2,128,64]{1,2,0:T(8,128)(2,1)}), bf16[2,128,64]{1,2,0:T(8,128)(2,1)S(1)}, u32[]{:S(2)}, u32[]{:S(2)}) %all-to-all-start.6) | async-done | bytes 32800 | tf_op jit(solution)/shard_map/all_to_all | solution.py:31
  260.1 1.2 gather_fusion.7
  (63 shorter events, 1.6 us)
Async XLA Ops:
  6.5 203.2 %copy-start = (bf16[128,8192]{1,0:T(8,128)(2,1)S(1)}, bf16[128,8192]{1,0:T(8,128)(2,1)}, u32[]{:S(2)}) copy-start(bf16[128,8192]{1,0:T(8,128)(2,1)} %param.33) | copy-start | bytes 6291460
  6.5 5.0 %copy-start.2 = (bf16[64,4096]{1,0:T(8,128)(2,1)S(1)}, bf16[64,4096]{1,0:T(8,128)(2,1)}, u32[]{:S(2)}) copy-start(bf16[64,4096]{1,0:T(8,128)(2,1)} %param.20) | copy-start | bytes 1572868
  6.5 6.0 %copy-start.15 = (s32[2]{0:T(128)S(1)}, s32[2]{0:T(128)}, u32[]{:S(2)}) copy-start(s32[2]{0:T(128)} %param.27) | copy-start | bytes 28
  12.4 17.6 %copy-start.9 = (s32[64,64]{1,0:T(8,128)S(1)}, s32[64,64]{1,0:T(8,128)}, u32[]{:S(2)}) copy-start(s32[64,64]{1,0:T(8,128)} %param.26) | copy-start | bytes 49156
  12.6 18.8 %copy-start.7 = (bf16[64,512]{1,0:T(8,128)(2,1)S(1)}, bf16[64,512]{1,0:T(8,128)(2,1)}, u32[]{:S(2)}) copy-start(bf16[64,512]{1,0:T(8,128)(2,1)} %param.21) | copy-start | bytes 196612
  17.5 32.7 %all-to-all-start.1 = ((f32[1,64,32]{2,0,1:T(1,128)}), f32[1,64,32]{2,0,1:T(1,128)S(1)}, u32[]{:S(2)}, u32[]{:S(2)}) async-start(f32[1,64,32]{2,0,1:T(1,128)} %copy.96), calls=%async_computation.1 | async-start | bytes 65536 | tf_op jit(solution)/shard_map/all_to_all | solution.py:160
  33.5 3.5 %copy-start.3 = (f32[2,4,32,8,512]{4,3,2,1,0:T(8,128)S(1)}, f32[2,4,32,8,512]{4,3,2,1,0:T(8,128)}, u32[]{:S(2)}) copy-start(f32[2,4,32,8,512]{4,3,2,1,0:T(8,128)} %get-tuple-element.19) | copy-start | bytes 12582916
  38.3 5.7 %copy-start.8 = (bf16[64,512]{1,0:T(8,128)(2,1)S(1)}, bf16[64,512]{1,0:T(8,128)(2,1)}, u32[]{:S(2)}) copy-start(bf16[64,512]{1,0:T(8,128)(2,1)} %param.22) | copy-start | bytes 196612
  50.2 40.8 %all-to-all-start = ((f32[1,2048,129]{2,0,1:T(1,128)}), f32[1,2048,129]{2,0,1:T(1,128)}, u32[]{:S(2)}, u32[]{:S(2)}) async-start(f32[1,2048,129]{2,0,1:T(1,128)} %copy.94), calls=%async_computation | async-start | bytes 4194304 | tf_op jit(solution)/shard_map/all_to_all | solution.py:18
  62.1 41.7 %copy-start.13 = (f32[2,4]{1,0:T(2,128)S(1)}, f32[2,4]{1,0:T(2,128)}, u32[]{:S(2)}) copy-start(f32[2,4]{1,0:T(2,128)} %param.37) | copy-start | bytes 100
  92.7 1.4 copy-start.4
  94.7 30.7 %copy-start.12 = (bf16[64,128]{1,0:T(8,128)(2,1)S(1)}, bf16[64,128]{1,0:T(8,128)(2,1)}, u32[]{:S(2)}) copy-start(bf16[64,128]{1,0:T(8,128)(2,1)} %param.19) | copy-start | bytes 49156
  95.0 48.4 %copy-start.14 = (f32[128]{0:T(128)S(1)}, f32[128]{0:T(128)}, u32[]{:S(2)}) copy-start(f32[128]{0:T(128)} %param.30) | copy-start | bytes 1540
  98.2 19.5 %all-to-all-start.2 = ((bf16[64,32,128]{2,1,0:T(8,128)(2,1)}), bf16[64,32,128]{2,1,0:T(8,128)(2,1)S(1)}, u32[]{:S(2)}, u32[]{:S(2)}) async-start(bf16[64,32,128]{2,1,0:T(8,128)(2,1)} %broadcast_in_dim.76), calls=%async_computation.2 | async-start | bytes 1048576 | tf_op jit(solution)/shard_map/all_to_all | solution.py:31
  122.2 7.2 %all-to-all-start.3 = ((bf16[2,64,128]{2,1,0:T(8,128)(2,1)}), bf16[2,64,128]{2,1,0:T(8,128)(2,1)S(1)}, u32[]{:S(2)}, u32[]{:S(2)}) async-start(bf16[2,64,128]{2,1,0:T(8,128)(2,1)} %broadcast_in_dim.77), calls=%async_computation.3 | async-start | bytes 65536 | tf_op jit(solution)/shard_map/all_to_all | solution.py:31
  125.4 76.3 %all-gather.2.cloned.1.call-start = ((), (), s32[]{:S(2)}) async-start(), calls=%async_computation.7 | async-start | bytes 1064960 | tf_op jit(solution)/shard_map/all_gather | solution.py:204
  201.8 3.4 %copy-start.1 = (bf16[64,8192]{1,0:T(8,128)(2,1)S(1)}, bf16[64,8192]{1,0:T(8,128)(2,1)}, u32[]{:S(2)}) copy-start(bf16[64,8192]{1,0:T(8,128)(2,1)} %all-gather.2.cloned.1.call-done) | copy-start | bytes 3145732
  201.8 4.1 %copy-start.5 = (bf16[2,8192,128]{2,1,0:T(8,128)(2,1)S(1)}, bf16[2,8192,128]{2,1,0:T(8,128)(2,1)}, u32[]{:S(2)}) copy-start(bf16[2,8192,128]{2,1,0:T(8,128)(2,1)} %param.34) | copy-start | bytes 12582916
  205.2 1.8 copy-start.10
  205.8 1.7 copy-start.11
  206.6 2.4 copy-start.6
  211.8 38.7 %all-to-all-start.5 = ((f32[64,128,64]{1,2,0:T(8,128)}), f32[64,128,64]{1,2,0:T(8,128)}, u32[]{:S(2)}, u32[]{:S(2)}) async-start(f32[64,128,64]{1,2,0:T(8,128)} %bitcast.112), calls=%async_computation.5 | async-start | bytes 4194304 | tf_op jit(solution)/shard_map/all_to_all | solution.py:61
  252.9 7.2 %all-to-all-start.6 = ((bf16[2,128,64]{1,2,0:T(8,128)(2,1)}), bf16[2,128,64]{1,2,0:T(8,128)(2,1)S(1)}, u32[]{:S(2)}, u32[]{:S(2)}) async-start(bf16[2,128,64]{1,2,0:T(8,128)(2,1)} %broadcast_in_dim.79), calls=%async_computation.6 | async-start | bytes 65536 | tf_op jit(solution)/shard_map/all_to_all | solution.py:31
Sparse Core Ops, SparseCore 0:
  144.2 57.4 all-gather.1
where the time goes:
time: 269 us; the launch traced here: 268 us
  waiting for transfers between devices  135 us (50%)
  starting transfers between devices  42.8 us (16%)
  local copies, waits for them, and re-layouts  27.9 us (10%)
  other arithmetic  17.5 us (7%)
  matrix products  16.8 us (6%)
  blocking collectives  13.8 us (5%)
  between operations  13.8 us (5%)
    all_gather x1, waiting for transfers between devices, shards(): piece = lax.all_gather(normed, 'ctx', axis=1, tiled=True)  57.7 us
    all_to_all x1, waiting for transfers between devices, sent_together(): lax.all_to_all(both, axis, split_axis=split_dim, concat_axis=concat_dim,...  28.9 us
    all_to_all x1, waiting for transfers between devices, sum_at_owner(): lax.all_to_all(tiles, axis, split_axis=0, concat_axis=0, tiled=True)  28.1 us
    all_to_all x3, waiting for transfers between devices, sent_to_all(): return lax.all_to_all(copies, axis, split_axis=0, concat_axis=0, tiled=True)  20.9 us
    all_to_all x1, blocking collectives, sent_to_all(): return lax.all_to_all(copies, axis, split_axis=0, concat_axis=0, tiled=True)  13.8 us
    all_to_all x3, starting transfers between devices, sent_to_all(): return lax.all_to_all(copies, axis, split_axis=0, concat_axis=0, tiled=True)  12.1 us
    all_to_all x1, starting transfers between devices, shards(): lax.all_to_all(part_top.reshape(1, all_rows), 'ctx', split_axis=1, concat...  11.5 us
    all_to_all x1, starting transfers between devices, sent_together(): lax.all_to_all(both, axis, split_axis=split_dim, concat_axis=concat_dim,...  10.6 us
  transfers between devices with their start and end apart: 7, of which 6 were waited for; matrix products, arithmetic and copies ran while one was open for 9% of the time, Pallas kernels for 0%

commit v1 on v0

--- a/solution.py
+++ b/solution.py
@@ -201,7 +201,9 @@
     squares = of_everyone_2(jnp.sum(hidden * hidden, axis=1), "ctx")
     normed = (hidden * lax.rsqrt(squares / D + EPS)[:, None] * norm_gain).astype(jnp.bfloat16)
     hidden_units = gate_weight.shape[1]
-    piece = lax.all_gather(normed, "ctx", axis=1, tiled=True)
+    piece = jnp.concatenate(
+        lax.all_to_all(jnp.stack([normed] * lax.axis_size("ctx")), "ctx", 0, 0), axis=1
+    )
     size = piece.shape[1]
     split_piece = piece.reshape(tenants, draft, size)
     gate_base = jnp.dot(piece, gate_weight, preferred_element_type=jnp.float32)

time: 269 us -> 223 us (0.83)
  waiting for transfers between devices: 135 us -> 77.9 us
  blocking collectives: 13.8 us -> 37.6 us
  between operations: 13.8 us -> 0.46 us
  local copies, waits for them, and re-layouts: 27.9 us -> 32.4 us
  starting transfers between devices: 42.8 us -> 39.8 us
    all_gather x1 -> x0, waiting for transfers between devices: 57.7 us -> none  [shards(): piece = lax.all_gather(normed, 'ctx', axis=1, tiled=True)]
    all_to_all x0 -> x1, blocking collectives: none -> 23.8 us  [shards(): lax.all_to_all(jnp.stack([normed] * lax.axis_size('ctx')), 'ctx', 0, 0)]
    all_to_all x1, starting transfers between devices: 8.58 us -> 5.56 us  [sum_at_owner(): lax.all_to_all(tiles, axis, split_axis=0, concat_axis=0, tiled=True)]
    unnamed x34 -> x36, local copies, waits for them, and re-layouts: 5.29 us -> 6.28 us
  transfers between devices with their start and end apart: 7 -> 6, of which waited for: 6 -> 5; matrix products, arithmetic and copies ran while one was open for 9% -> 11% of each run, Pallas kernels for 0% -> 0%
where the time goes in v1:
time: 223 us; the launch traced here: 222 us
  waiting for transfers between devices  77.9 us (35%)
  starting transfers between devices  39.8 us (18%)
  blocking collectives  37.6 us (17%)
  local copies, waits for them, and re-layouts  32.4 us (15%)
  other arithmetic  16.9 us (8%)
  matrix products  16.6 us (7%)
    all_to_all x1, waiting for transfers between devices, sent_together(): lax.all_to_all(both, axis, split_axis=split_dim, concat_axis=concat_dim,...  28.9 us
    all_to_all x1, waiting for transfers between devices, sum_at_owner(): lax.all_to_all(tiles, axis, split_axis=0, concat_axis=0, tiled=True)  28.1 us
    all_to_all x1, blocking collectives, shards(): lax.all_to_all(jnp.stack([normed] * lax.axis_size('ctx')), 'ctx', 0, 0)  23.8 us
    all_to_all x3, waiting for transfers between devices, sent_to_all(): return lax.all_to_all(copies, axis, split_axis=0, concat_axis=0, tiled=True)  20.9 us
    all_to_all x1, blocking collectives, sent_to_all(): return lax.all_to_all(copies, axis, split_axis=0, concat_axis=0, tiled=True)  13.9 us
    all_to_all x3, starting transfers between devices, sent_to_all(): return lax.all_to_all(copies, axis, split_axis=0, concat_axis=0, tiled=True)  12.1 us
    all_to_all x1, starting transfers between devices, shards(): lax.all_to_all(part_top.reshape(1, all_rows), 'ctx', split_axis=1, concat...  11.5 us
    all_to_all x1, starting transfers between devices, sent_together(): lax.all_to_all(both, axis, split_axis=split_dim, concat_axis=concat_dim,...  10.6 us
  transfers between devices with their start and end apart: 6, of which 5 were waited for; matrix products, arithmetic and copies ran while one was open for 11% of the time, Pallas kernels for 0%

profile of v1, /device:TPU:0, one launch (start us, length us, event | category | flops | bytes accessed | tf_op | source)
XLA Modules:
  0.0 221.5 jit_solution(11853324254874549919)
XLA Ops:
  0.0 2.8 %sort.34 = (s32[64]{0:T(128)}, s32[64]{0:T(128)S(1)}) sort(s32[64]{0:T(128)} %param.25, s32[64]{0:T(128)S(1)} %iota.25), dimensions={0}, to_apply=%region_0.0 | sort | flops 384 | bytes 1024 | tf_op jit(solution)/shard_map/jit(argsort)/sort | solution.py:125
  2.9 2.2 reshape.272
  5.0 0.9 gather_fusion.1
  6.1 4.0 %bitcast_reduce_fusion = (f32[2,32,4,8]{3,1,2,0:T(8,128)S(1)}, f32[2,4,32,8,512]{4,3,2,1,0:T(8,128)}) fusion(pred[2,512]{1,0:T(4,128)(4,1)S(1)} %broadcast_compare_fusion, bf16[2,512,4,128,1]{3,2,1,0,4:T(4,128)(2,1)} %bitcast.126, bf16[2,32,4,8,128]{4,3,2,1,0:T(8,128)(2,1)S(1)} %bitcast.128), kind=kOutput, calls=%fused_computation.12 | convolution fusion | flops 271579136 | bytes 5776384 | tf_op jit(solution)/shard_map/tqgwd,tjgd->tqgwj/dot_general | solution.py:138
  10.3 0.7 copy.101
  11.0 11.5 %all-to-all-start.1 = ((f32[1,64,32]{2,0,1:T(1,128)}), f32[1,64,32]{2,0,1:T(1,128)S(1)}, u32[]{:S(2)}, u32[]{:S(2)}) async-start(f32[1,64,32]{2,0,1:T(1,128)} %copy.101), calls=%async_computation.1 | async-start | bytes 65536 | tf_op jit(solution)/shard_map/all_to_all | solution.py:160
  22.5 1.0 reshape.275
  23.5 0.6 gather_fusion.2
  24.2 0.6 gather_fusion.3
  24.9 0.7 gather_fusion.5
  25.6 1.3 reshape.273
  26.9 3.5 %fusion.4 = f32[2,32,4,8]{3,1,2,0:T(8,128)S(1)} fusion(f32[2,4,32,8,512]{4,3,2,1,0:T(8,128)} %get-tuple-element.19, f32[2,32,4,8]{3,1,2,0:T(8,128)S(1)} %get-tuple-element.18, pred[2,512]{1,0:T(4,128)(4,1)S(1)} %broadcast_compare_fusion), kind=kLoop, calls=%fused_computation.17 | loop fusion | flops 5240832 | bytes 4211712 | tf_op jit(solution)/shard_map/reduce_sum | solution.py:146
  30.5 1.3 fusion.10
  32.0 1.3 reshape_reshape_reshape.8
  33.4 3.2 %pad_maximum_fusion = f32[1,2048,129]{2,1,0:T(8,128)} fusion(f32[1,2048,128]{2,1,0:T(8,128)S(1)} %bitcast.127, f32[1,2048,1]{2,1,0:T(8,128)} %reshape_reshape_reshape.8), kind=kLoop, calls=%fused_computation.19 | loop fusion | flops 264192 | bytes 2113536 | tf_op jit(solution)/shard_map/concatenate | solution.py:16
  36.5 0.8 fusion.13
  37.5 0.7 gather_fusion.6
  38.2 4.8 %copy.99 = f32[1,2048,129]{2,0,1:T(1,128)} copy(f32[1,2048,129]{2,1,0:T(8,128)} %pad_maximum_fusion) | data formatting | bytes 2113536 | tf_op jit(solution)/shard_map/concatenate | solution.py:16
  43.0 0.6 gather_fusion.4
  43.6 10.6 %all-to-all-start = ((f32[1,2048,129]{2,0,1:T(1,128)}), f32[1,2048,129]{2,0,1:T(1,128)}, u32[]{:S(2)}, u32[]{:S(2)}) async-start(f32[1,2048,129]{2,0,1:T(1,128)} %copy.99), calls=%async_computation | async-start | bytes 4194304 | tf_op jit(solution)/shard_map/all_to_all | solution.py:18
  54.3 0.3 fusion.35
  54.7 0.2 fusion.43
  54.9 0.2 fusion.28
  55.1 0.3 fusion.33
  55.6 28.9 %all-to-all-done = f32[1,2048,129]{2,0,1:T(1,128)} async-done(((f32[1,2048,129]{2,0,1:T(1,128)}), f32[1,2048,129]{2,0,1:T(1,128)}, u32[]{:S(2)}, u32[]{:S(2)}) %all-to-all-start) | async-done | bytes 1056800 | tf_op jit(solution)/shard_map/all_to_all | solution.py:18
  84.4 1.7 copy.125
  86.2 1.3 copy-done.5
  87.6 0.6 copy.108
  88.5 2.2 fusion.19
  90.8 0.9 broadcast_in_dim.76
  91.7 5.5 %all-to-all-start.2 = ((bf16[64,32,128]{2,1,0:T(8,128)(2,1)}), bf16[64,32,128]{2,1,0:T(8,128)(2,1)S(1)}, u32[]{:S(2)}, u32[]{:S(2)}) async-start(bf16[64,32,128]{2,1,0:T(8,128)(2,1)} %broadcast_in_dim.76), calls=%async_computation.2 | async-start | bytes 1048576 | tf_op jit(solution)/shard_map/all_to_all | solution.py:31
  97.2 0.2 multiply_reduce_fusion.1
  97.5 13.7 %all-to-all-done.2 = bf16[64,32,128]{2,1,0:T(8,128)(2,1)S(1)} async-done(((bf16[64,32,128]{2,1,0:T(8,128)(2,1)}), bf16[64,32,128]{2,1,0:T(8,128)(2,1)S(1)}, u32[]{:S(2)}, u32[]{:S(2)}) %all-to-all-start.2) | async-done | bytes 524320 | tf_op jit(solution)/shard_map/all_to_all | solution.py:31
  111.2 0.2 reshape_reshape_reshape.7
  111.4 2.0 convolution_multiply_fusion.4
  113.4 1.6 fusion.16
  115.0 0.6 broadcast_in_dim.77
  115.6 3.3 %all-to-all-start.3 = ((bf16[2,64,128]{2,1,0:T(8,128)(2,1)}), bf16[2,64,128]{2,1,0:T(8,128)(2,1)S(1)}, u32[]{:S(2)}, u32[]{:S(2)}) async-start(bf16[2,64,128]{2,1,0:T(8,128)(2,1)} %broadcast_in_dim.77), calls=%async_computation.3 | async-start | bytes 65536 | tf_op jit(solution)/shard_map/all_to_all | solution.py:31
  118.9 0.6 gather_fusion
  119.6 3.3 %all-to-all-done.3 = bf16[2,64,128]{2,1,0:T(8,128)(2,1)S(1)} async-done(((bf16[2,64,128]{2,1,0:T(8,128)(2,1)}), bf16[2,64,128]{2,1,0:T(8,128)(2,1)S(1)}, u32[]{:S(2)}, u32[]{:S(2)}) %all-to-all-start.3) | async-done | bytes 32800 | tf_op jit(solution)/shard_map/all_to_all | solution.py:31
  123.0 13.9 %all_to_all.59 = f32[64,1,64]{2,1,0:T(1,128)S(1)} all-to-all(f32[64,1,64]{2,1,0:T(1,128)S(1)} %broadcast_in_dim.78), channel_id=1, replica_groups=mesh['kv'=2,'ctx'=64] {'ctx'}, dimensions={0} | all-to-all | bytes 32768 | tf_op jit(solution)/shard_map/all_to_all | solution.py:31
  137.0 0.2 stack.2
  137.2 23.8 %all_to_all.60 = bf16[64,64,128]{2,1,0:T(8,128)(2,1)S(1)} all-to-all(bf16[64,64,128]{2,1,0:T(8,128)(2,1)S(1)} %stack.2), channel_id=1, replica_groups=mesh['kv'=2,'ctx'=64] {'ctx'}, dimensions={0} | all-to-all | bytes 2097152 | tf_op jit(solution)/shard_map/all_to_all | solution.py:205
  161.0 1.0 copy-done.3
  162.0 1.7 copy.110
  163.7 1.5 reshape_reshape.12
  165.2 3.1 %convolution_multiply_fusion.2 = f32[2,32,128]{2,1,0:T(8,128)S(1)} fusion(bf16[2,32,8192]{2,1,0:T(8,128)(2,1)S(1)} %reshape_reshape.12, bf16[2,8192,128]{2,1,0:T(8,128)(2,1)} %param.35, f32[2]{0:T(128)S(1)} %get-tuple-element.12), kind=kOutput, calls=%fused_computation.27 | convolution fusion | flops 134225920 | bytes 5275656 | tf_op jit(solution)/shard_map/tqf,tfh->tqh/dot_general | solution.py:214
  168.3 0.3 copy-done.6
  168.6 0.8 convolution_multiply_fusion.3
  169.6 0.7 copy-done.11
  170.3 0.5 convolution_add_fusion.1
  170.9 0.5 fusion.15
  171.4 0.8 copy-done.7
  172.3 0.7 convolution_multiply_fusion
  173.0 0.5 fusion.9
  173.5 1.6 copy.172
  175.0 5.6 %all-to-all-start.6 = ((f32[64,128,64]{1,2,0:T(8,128)}), f32[64,128,64]{1,2,0:T(8,128)}, u32[]{:S(2)}, u32[]{:S(2)}) async-start(f32[64,128,64]{1,2,0:T(8,128)} %bitcast.121), calls=%async_computation.6 | async-start | bytes 4194304 | tf_op jit(solution)/shard_map/all_to_all | solution.py:61
  180.6 2.0 sort.35
  182.7 28.1 %all-to-all-done.6 = f32[64,128,64]{1,2,0:T(8,128)} async-done(((f32[64,128,64]{1,2,0:T(8,128)}), f32[64,128,64]{1,2,0:T(8,128)}, u32[]{:S(2)}, u32[]{:S(2)}) %all-to-all-start.6) | async-done | bytes 2097184 | tf_op jit(solution)/shard_map/all_to_all | solution.py:61
  210.8 1.7 reduce_sum.88
  212.5 0.6 broadcast_in_dim.79
  213.1 3.3 %all-to-all-start.7 = ((bf16[2,128,64]{1,2,0:T(8,128)(2,1)}), bf16[2,128,64]{1,2,0:T(8,128)(2,1)S(1)}, u32[]{:S(2)}, u32[]{:S(2)}) async-start(bf16[2,128,64]{1,2,0:T(8,128)(2,1)} %broadcast_in_dim.79), calls=%async_computation.7 | async-start | bytes 65536 | tf_op jit(solution)/shard_map/all_to_all | solution.py:31
  216.4 3.9 %all-to-all-done.7 = bf16[2,128,64]{1,2,0:T(8,128)(2,1)S(1)} async-done(((bf16[2,128,64]{1,2,0:T(8,128)(2,1)}), bf16[2,128,64]{1,2,0:T(8,128)(2,1)S(1)}, u32[]{:S(2)}, u32[]{:S(2)}) %all-to-all-start.7) | async-done | bytes 32800 | tf_op jit(solution)/shard_map/all_to_all | solution.py:31
  220.3 1.2 gather_fusion.7
  (66 shorter events, 2.2 us)
Async XLA Ops:
  0.0 172.9 %copy-start = (bf16[128,8192]{1,0:T(8,128)(2,1)S(1)}, bf16[128,8192]{1,0:T(8,128)(2,1)}, u32[]{:S(2)}) copy-start(bf16[128,8192]{1,0:T(8,128)(2,1)} %param.33) | copy-start | bytes 6291460
  0.0 5.0 %copy-start.1 = (bf16[64,4096]{1,0:T(8,128)(2,1)S(1)}, bf16[64,4096]{1,0:T(8,128)(2,1)}, u32[]{:S(2)}) copy-start(bf16[64,4096]{1,0:T(8,128)(2,1)} %param.20) | copy-start | bytes 1572868
  0.0 6.0 %copy-start.16 = (s32[2]{0:T(128)S(1)}, s32[2]{0:T(128)}, u32[]{:S(2)}) copy-start(s32[2]{0:T(128)} %param.27) | copy-start | bytes 28
  5.9 17.6 %copy-start.10 = (s32[64,64]{1,0:T(8,128)S(1)}, s32[64,64]{1,0:T(8,128)}, u32[]{:S(2)}) copy-start(s32[64,64]{1,0:T(8,128)} %param.26) | copy-start | bytes 49156
  6.0 18.8 %copy-start.8 = (bf16[64,512]{1,0:T(8,128)(2,1)S(1)}, bf16[64,512]{1,0:T(8,128)(2,1)}, u32[]{:S(2)}) copy-start(bf16[64,512]{1,0:T(8,128)(2,1)} %param.21) | copy-start | bytes 196612
  11.0 32.7 %all-to-all-start.1 = ((f32[1,64,32]{2,0,1:T(1,128)}), f32[1,64,32]{2,0,1:T(1,128)S(1)}, u32[]{:S(2)}, u32[]{:S(2)}) async-start(f32[1,64,32]{2,0,1:T(1,128)} %copy.101), calls=%async_computation.1 | async-start | bytes 65536 | tf_op jit(solution)/shard_map/all_to_all | solution.py:160
  26.9 3.5 %copy-start.2 = (f32[2,4,32,8,512]{4,3,2,1,0:T(8,128)S(1)}, f32[2,4,32,8,512]{4,3,2,1,0:T(8,128)}, u32[]{:S(2)}) copy-start(f32[2,4,32,8,512]{4,3,2,1,0:T(8,128)} %get-tuple-element.19) | copy-start | bytes 12582916
  31.8 5.7 %copy-start.9 = (bf16[64,512]{1,0:T(8,128)(2,1)S(1)}, bf16[64,512]{1,0:T(8,128)(2,1)}, u32[]{:S(2)}) copy-start(bf16[64,512]{1,0:T(8,128)(2,1)} %param.22) | copy-start | bytes 196612
  43.6 40.8 %all-to-all-start = ((f32[1,2048,129]{2,0,1:T(1,128)}), f32[1,2048,129]{2,0,1:T(1,128)}, u32[]{:S(2)}, u32[]{:S(2)}) async-start(f32[1,2048,129]{2,0,1:T(1,128)} %copy.99), calls=%async_computation | async-start | bytes 4194304 | tf_op jit(solution)/shard_map/all_to_all | solution.py:18
  55.5 41.7 %copy-start.14 = (f32[2,4]{1,0:T(2,128)S(1)}, f32[2,4]{1,0:T(2,128)}, u32[]{:S(2)}) copy-start(f32[2,4]{1,0:T(2,128)} %param.37) | copy-start | bytes 100
  86.1 1.4 copy-start.5
  88.2 30.7 %copy-start.13 = (bf16[64,128]{1,0:T(8,128)(2,1)S(1)}, bf16[64,128]{1,0:T(8,128)(2,1)}, u32[]{:S(2)}) copy-start(bf16[64,128]{1,0:T(8,128)(2,1)} %param.19) | copy-start | bytes 49156
  88.5 48.4 %copy-start.15 = (f32[128]{0:T(128)S(1)}, f32[128]{0:T(128)}, u32[]{:S(2)}) copy-start(f32[128]{0:T(128)} %param.30) | copy-start | bytes 1540
  91.7 19.5 %all-to-all-start.2 = ((bf16[64,32,128]{2,1,0:T(8,128)(2,1)}), bf16[64,32,128]{2,1,0:T(8,128)(2,1)S(1)}, u32[]{:S(2)}, u32[]{:S(2)}) async-start(bf16[64,32,128]{2,1,0:T(8,128)(2,1)} %broadcast_in_dim.76), calls=%async_computation.2 | async-start | bytes 1048576 | tf_op jit(solution)/shard_map/all_to_all | solution.py:31
  115.6 7.2 %all-to-all-start.3 = ((bf16[2,64,128]{2,1,0:T(8,128)(2,1)}), bf16[2,64,128]{2,1,0:T(8,128)(2,1)S(1)}, u32[]{:S(2)}, u32[]{:S(2)}) async-start(bf16[2,64,128]{2,1,0:T(8,128)(2,1)} %broadcast_in_dim.77), calls=%async_computation.3 | async-start | bytes 65536 | tf_op jit(solution)/shard_map/all_to_all | solution.py:31
  161.0 1.0 copy-start.3
  165.2 3.5 %copy-start.6 = (bf16[2,8192,128]{2,1,0:T(8,128)(2,1)S(1)}, bf16[2,8192,128]{2,1,0:T(8,128)(2,1)}, u32[]{:S(2)}) copy-start(bf16[2,8192,128]{2,1,0:T(8,128)(2,1)} %param.34) | copy-start | bytes 12582916
  168.3 1.3 copy-start.4
  168.3 2.0 copy-start.11
  168.6 2.2 %copy-start.12 = (bf16[8192,128]{1,0:T(8,128)(2,1)S(1)}, bf16[8192,128]{1,0:T(8,128)(2,1)}, u32[]{:S(2)}) copy-start(bf16[8192,128]{1,0:T(8,128)(2,1)} %param.32) | copy-start | bytes 6291460
  169.4 2.8 %copy-start.7 = (bf16[2,128,8192]{2,1,0:T(8,128)(2,1)S(1)}, bf16[2,128,8192]{2,1,0:T(8,128)(2,1)}, u32[]{:S(2)}) copy-start(bf16[2,128,8192]{2,1,0:T(8,128)(2,1)} %param.36) | copy-start | bytes 12582916
  175.0 35.7 %all-to-all-start.6 = ((f32[64,128,64]{1,2,0:T(8,128)}), f32[64,128,64]{1,2,0:T(8,128)}, u32[]{:S(2)}, u32[]{:S(2)}) async-start(f32[64,128,64]{1,2,0:T(8,128)} %bitcast.121), calls=%async_computation.6 | async-start | bytes 4194304 | tf_op jit(solution)/shard_map/all_to_all | solution.py:61
  213.1 7.2 %all-to-all-start.7 = ((bf16[2,128,64]{1,2,0:T(8,128)(2,1)}), bf16[2,128,64]{1,2,0:T(8,128)(2,1)S(1)}, u32[]{:S(2)}, u32[]{:S(2)}) async-start(bf16[2,128,64]{1,2,0:T(8,128)(2,1)} %broadcast_in_dim.79), calls=%async_computation.7 | async-start | bytes 65536 | tf_op jit(solution)/shard_map/all_to_all | solution.py:31
